TPU v7x, 32 devices: a whole 2x2x4 slice. The times are simulated.
32 devices in a mesh: parts: 2 (over y), blk: 4 (over z), row: 2 (over x), sub: 2 (over core).
Axes of the slice: x: 2, y: 2, z: 4, core: 2. Of those that a mesh axis runs over, the one named last changes fastest.
Arguments:
- query_grads: bfloat16 [512, 4, 2048], P('blk', None, 'sub'), may hold values from -6 to 6
- curvature: bfloat16 [4, 2048, 2048], P('blk', ('row', 'sub')), may hold values from -0.125 to 0.125
- train_grads: bfloat16 [5120, 4, 2048], P(('parts', 'row', 'sub'), 'blk'), parts along dimension 0, may hold values from -0.0625 to 0.0625
- query_ids: int32 [1024], P('parts'), parts along dimension 0, may hold values from 0 to 511, each once
- block_map: int32 [4], replicated, may hold values from 0 to 3, each once
- row_ids: int32 [5120], P(('parts', 'row', 'sub')), parts along dimension 0, may hold values from 0 to 639
Outputs:
- scores: float32 [512, 5120], P('blk', ('parts', 'row', 'sub')), parts along dimension 1
There are 2 independent parts, one for each index of `parts`. A program takes and returns all parts, laid end to end along the dimension named above; an argument that names none is the same for every part. Nothing has to cross between parts.
Inputs may be any that keep to these rules, and one draw needn't show every extreme that they name: `query_ids`: each value appears once. `block_map`: each value appears once.
All inputs are finite; a program needn't handle non-finite values.
Results may differ from a plain program's by a relative error of at most 0.0029.
Values may be sent and summed in bfloat16 or wider, within the bound.
No kernel may reach another device: no remote copies, remote signals or barrier semaphores. Data moves between devices by JAX's collectives and lax.ppermute only.
A program may use at most 64 MiB of HBM per device.

v0:
```python
import jax
import jax.numpy as jnp
from jax import lax
from jax.sharding import PartitionSpec as P


def per_device(query_grads, curvature, train_grads, query_ids, block_map, row_ids):
    mine = jnp.take(query_grads, block_map, axis=1)
    arrived = lax.all_to_all(mine, "blk", split_axis=1, concat_axis=0, tiled=True)
    queries = arrived.shape[0]
    precond = jnp.einsum(
        "qsj,sij->qsi",
        lax.all_gather(arrived, "sub", axis=2, tiled=True),
        curvature,
        preferred_element_type=jnp.float32,
    ).astype(jnp.bfloat16)
    inverse = (
        jnp.zeros((queries,), jnp.int32).at[query_ids].set(jnp.arange(queries, dtype=jnp.int32))
    )
    ordered = jnp.take(precond, inverse, axis=0)
    chosen = jnp.take(train_grads, row_ids, axis=0)
    partial_value = jnp.einsum(
        "qsk,rsk->qr",
        lax.all_gather(ordered, ("row", "sub"), axis=2, tiled=True),
        chosen,
        preferred_element_type=jnp.float32,
    )
    return lax.psum_scatter(partial_value, "blk", scatter_dimension=0, tiled=True)


def solution(mesh):
    placed = (
        P("blk", None, "sub"),
        P("blk", ("row", "sub"), None),
        P(("parts", "row", "sub"), "blk", None),
        P("parts"),
        P(),
        P(("parts", "row", "sub")),
    )
    return jax.shard_map(
        per_device,
        mesh=mesh,
        in_specs=placed,
        out_specs=P("blk", ("parts", "row", "sub")),
        check_vma=False,
    )
```

profile of v0, /device:TPU:0, one launch (start us, length us, event | category | flops | bytes accessed | tf_op | source)
XLA Modules:
  0.0 133.5 jit_solution(11992758323479835850)
XLA Ops:
  6.5 0.8 compare_and_fusion.1
  7.4 0.7 compare_select_fusion.3
  8.0 6.1 %gather_fusion = bf16[4,128,1024]{2,0,1:T(4,128)(2,1)} fusion(bf16[128,4,1024]{2,1,0:T(4,128)(2,1)} %param.6, s32[1024]{0:T(1024)S(1)} %pad_clamp_fusion.2), kind=kCustom, calls=%fused_computation | custom fusion | bytes 2097168 | tf_op jit(solution)/shard_map/jit(_take)/gather | solution.py:8
  14.1 1.7 %select_bitcast_fusion = bf16[128,4,1024]{2,1,0:T(4,128)(2,1)S(1)} fusion(bf16[4,128,1024]{2,0,1:T(4,128)(2,1)} %gather_fusion, pred[4]{0:T(512)(128)(4,1)S(1)} %compare_and_fusion.1), kind=kLoop, calls=%fused_computation.14 | loop fusion | flops 524288 | bytes 2097156 | tf_op jit(solution)/shard_map/jit(_take)/select_n | solution.py:8
  15.9 0.3 copy.8
  16.2 0.0 copy-start.2
  16.2 32.0 %all_to_all.18 = bf16[128,4,1024]{2,0,1:T(8,128)(2,1)} all-to-all(bf16[128,4,1024]{2,0,1:T(8,128)(2,1)S(1)} %copy.8), channel_id=1, replica_groups=mesh['parts'=2,'blk'=4,'row'=2,'sub'=2] {'blk'}, dimensions={1} | all-to-all | bytes 2097152 | tf_op jit(solution)/shard_map/all_to_all | solution.py:9
  48.2 0.0 all-gather.3.cloned.1.call-update
  48.2 0.0 all-gather.5.cloned.1.call-start
  48.2 0.0 copy-done.2
  48.3 2.4 %scatter_custom_fusion = s32[512]{0:T(512)S(1)} fusion(s32[512]{0:T(512)S(1)} %compare_select_fusion.2, s32[512]{0:T(512)S(1)} %iota.3, s32[]{:T(128)} %constant.30.clone.1), kind=kCustom, calls=%fused_computation.26 | custom fusion | bytes 2052 | tf_op jit(solution)/shard_map/scatter | solution.py:18
  50.8 7.3 %all-gather.3.cloned.1.call-done = bf16[512,1,2048]{2,0,1:T(8,128)(2,1)} async-done(((bf16[512,1,1024]{2,0,1:T(8,128)(2,1)}), bf16[512,1,2048]{2,0,1:T(8,128)(2,1)}) %all-gather.3.cloned.1.call-update) | async-done | bytes 2097168 | tf_op jit(solution)/shard_map/all_gather | solution.py:13
  58.0 3.5 %fusion.8 = bf16[512,512]{1,0:T(8,128)(2,1)S(1)} fusion(bf16[1,512,2048]{2,1,0:T(8,128)(2,1)} %param.7, bf16[512,1,2048]{2,0,1:T(8,128)(2,1)} %all-gather.3.cloned.1.call-done), kind=kOutput, calls=%fused_computation.13 | convolution fusion | flops 1074003968 | bytes 4718592 | tf_op jit(solution)/shard_map/qsj,sij->qsi/dot_general | solution.py:11
  61.5 0.0 copy-start.1
  61.6 2.6 %gather_fusion.1 = bf16[512,512]{1,0:T(8,128)(2,1)} fusion(bf16[512,512]{1,0:T(8,128)(2,1)S(1)} %fusion.8, s32[1024]{0:T(1024)S(1)} %pad_clamp_fusion.1), kind=kCustom, calls=%fused_computation.1 | custom fusion | bytes 1050624 | tf_op jit(solution)/shard_map/jit(_take)/gather | solution.py:20
  64.2 2.0 %bitcast_select_fusion.2 = bf16[512,1,512]{2,0,1:T(8,128)(2,1)} fusion(bf16[512,512]{1,0:T(8,128)(2,1)} %gather_fusion.1, pred[512]{0:T(512)(128)(4,1)S(1)} %compare_and_fusion.2), kind=kLoop, calls=%fused_computation.15 | loop fusion | flops 262144 | bytes 1049088 | tf_op jit(solution)/shard_map/jit(_take)/select_n | solution.py:20
  66.2 0.0 all-gather.5.cloned.1.call-update
  66.2 0.0 reduce-scatter.2.cloned.1.call-start
  66.3 0.0 copy-done
  66.3 4.1 %gather_fusion.2 = bf16[640,2048]{1,0:T(8,128)(2,1)} fusion(bf16[640,2048]{1,0:T(8,128)(2,1)S(1)} %bitcast.32, s32[1024]{0:T(1024)S(1)} %pad_clamp_fusion), kind=kCustom, calls=%fused_computation.2 | custom fusion | bytes 5245440 | tf_op jit(solution)/shard_map/jit(_take)/gather | solution.py:21
  70.3 19.7 %all-gather.5.cloned.1.call-done = bf16[512,1,2048]{2,0,1:T(8,128)(2,1)} async-done(((bf16[512,1,512]{2,0,1:T(8,128)(2,1)}), bf16[512,1,2048]{2,0,1:T(8,128)(2,1)}) %all-gather.5.cloned.1.call-update) | async-done | bytes 2097168 | tf_op jit(solution)/shard_map/all_gather | solution.py:24
  90.1 5.4 %fusion = f32[512,640]{1,0:T(8,128)} fusion(bf16[640,2048]{1,0:T(8,128)(2,1)} %gather_fusion.2, pred[640]{0:T(1024)(128)(4,1)S(1)} %compare_and_fusion, bf16[512,1,2048]{2,0,1:T(8,128)(2,1)} %all-gather.5.cloned.1.call-done), kind=kOutput, calls=%fused_computation.4 | convolution fusion | flops 1343488000 | bytes 6029952 | tf_op jit(solution)/shard_map/qsk,rsk->qr/dot_general | solution.py:22
  95.5 0.0 reduce-scatter.2.cloned.1.call-update
  95.5 31.5 %reduce-scatter.2.cloned.1.call-done = f32[128,640]{1,0:T(8,128)} async-done(((f32[512,640]{1,0:T(8,128)}), f32[128,640]{1,0:T(8,128)}) %reduce-scatter.2.cloned.1.call-update) | async-done | bytes 327696 | tf_op jit(solution)/shard_map/reduce_scatter | solution.py:28
  (12 shorter events, 0.1 us)
Async XLA Ops:
  6.5 59.7 %copy-start = (bf16[640,1,2048]{2,0,1:T(8,128)(2,1)S(1)}, bf16[640,1,2048]{2,0,1:T(8,128)(2,1)}, u32[]{:S(2)}) copy-start(bf16[640,1,2048]{2,0,1:T(8,128)(2,1)} %param.8) | copy-start | bytes 7864324
  6.5 51.5 %all-gather.3.cloned.1.call-start = ((), (), s32[]{:S(2)}) async-start(), calls=%async_computation.2 | async-start | bytes 3145728 | tf_op jit(solution)/shard_map/all_gather | solution.py:13
  16.2 32.1 %copy-start.2 = (s32[512]{0:T(512)S(1)}, s32[512]{0:T(512)}, u32[]{:S(2)}) copy-start(s32[512]{0:T(512)} %param.9) | copy-start | bytes 6148
  48.2 41.9 %all-gather.5.cloned.1.call-start = ((), (), s32[]{:S(2)}) async-start(), calls=%async_computation.3 | async-start | bytes 2621440 | tf_op jit(solution)/shard_map/all_gather | solution.py:24
  61.5 4.7 %copy-start.1 = (s32[640]{0:T(1024)S(1)}, s32[640]{0:T(1024)}, u32[]{:S(2)}) copy-start(s32[640]{0:T(1024)} %param.11) | copy-start | bytes 7684
  66.2 60.8 %reduce-scatter.2.cloned.1.call-start = ((), (), s32[]{:S(2)}) async-start(), calls=%async_computation.4 | async-start | bytes 1638400 | tf_op jit(solution)/shard_map/reduce_scatter | solution.py:28
Sparse Core Ops, SparseCore 0:
  48.3 9.6 all-gather.2
  66.3 23.7 all-gather.4
  95.6 31.3 reduce-scatter.1
where the time goes:
time: 134 us
  waiting for transfers between devices  58.6 us (44%)
  blocking collectives  32 us (24%)
  local copies, waits for them, and re-layouts  15.6 us (12%)
  between operations  13.2 us (10%)
  matrix products  8.89 us (7%)
  other arithmetic  5.23 us (4%)
    all_to_all x1, blocking collectives, per_device(): lax.all_to_all(mine, 'blk', split_axis=1, concat_axis=0, tiled=True)  32 us
    reduce_scatter x1, waiting for transfers between devices, per_device(): lax.psum_scatter(partial_value, 'blk', scatter_dimension=0, tiled=True)  31.5 us
    all_gather x1, waiting for transfers between devices, per_device(): lax.all_gather(ordered, ('row', 'sub'), axis=2, tiled=True)  19.7 us
    all_gather x1, waiting for transfers between devices, per_device(): lax.all_gather(arrived, 'sub', axis=2, tiled=True)  7.27 us
    gather x1, local copies, waits for them, and re-layouts, per_device(): mine = jnp.take(query_grads, block_map, axis=1)  6.1 us
    dot_general x1, matrix products, per_device(): jnp.einsum('qsk,rsk->qr', lax.all_gather(ordered, ('row', 'sub'), axis=2,...  5.39 us
    gather x1, local copies, waits for them, and re-layouts, per_device(): chosen = jnp.take(train_grads, row_ids, axis=0)  4.06 us
    dot_general x1, matrix products, per_device(): jnp.einsum('qsj,sij->qsi', lax.all_gather(arrived, 'sub', axis=2, tiled=T...  3.5 us
  transfers between devices with their start and end apart: 3, of which 3 were waited for; matrix products, arithmetic and copies ran while one was open for 5% of the time, Pallas kernels for 0%

commit v1 on v0

--- a/solution.py
+++ b/solution.py
@@ -6,7 +6,10 @@
 
 def per_device(query_grads, curvature, train_grads, query_ids, block_map, row_ids):
     mine = jnp.take(query_grads, block_map, axis=1)
-    arrived = lax.all_to_all(mine, "blk", split_axis=1, concat_axis=0, tiled=True)
+    arrived = jnp.concatenate(
+        lax.all_to_all(jnp.stack(jnp.split(mine, lax.axis_size("blk"), axis=1)), "blk", 0, 0),
+        axis=0,
+    )
     queries = arrived.shape[0]
     precond = jnp.einsum(
         "qsj,sij->qsi",

time: 134 us -> 136 us (1.015)
  local copies, waits for them, and re-layouts: 15.6 us -> 17.2 us
    split x0 -> x1, local copies, waits for them, and re-layouts: none -> 1.55 us  [per_device(): jnp.split(mine, lax.axis_size('blk'), axis=1)]
where the time goes in v1:
time: 136 us; the launch traced here: 135 us
  waiting for transfers between devices  58.5 us (43%)
  blocking collectives  32 us (24%)
  local copies, waits for them, and re-layouts  17.2 us (13%)
  between operations  13.2 us (10%)
  matrix products  8.89 us (7%)
  other arithmetic  5.37 us (4%)
    all_to_all x1, blocking collectives, per_device(): lax.all_to_all(jnp.stack(jnp.split(mine, lax.axis_size('blk'), axis=1)),...  32 us
    reduce_scatter x1, waiting for transfers between devices, per_device(): lax.psum_scatter(partial_value, 'blk', scatter_dimension=0, tiled=True)  31.5 us
    all_gather x1, waiting for transfers between devices, per_device(): lax.all_gather(ordered, ('row', 'sub'), axis=2, tiled=True)  19.7 us
    all_gather x1, waiting for transfers between devices, per_device(): lax.all_gather(arrived, 'sub', axis=2, tiled=True)  7.27 us
    gather x1, local copies, waits for them, and re-layouts, per_device(): mine = jnp.take(query_grads, block_map, axis=1)  6.11 us
    dot_general x1, matrix products, per_device(): jnp.einsum('qsk,rsk->qr', lax.all_gather(ordered, ('row', 'sub'), axis=2,...  5.38 us
    gather x1, local copies, waits for them, and re-layouts, per_device(): chosen = jnp.take(train_grads, row_ids, axis=0)  4.08 us
    dot_general x1, matrix products, per_device(): jnp.einsum('qsj,sij->qsi', lax.all_gather(arrived, 'sub', axis=2, tiled=T...  3.5 us
  transfers between devices with their start and end apart: 3, of which 3 were waited for; matrix products, arithmetic and copies ran while one was open for 5% of the time, Pallas kernels for 0%

profile of v1, /device:TPU:0, one launch (start us, length us, event | category | flops | bytes accessed | tf_op | source)
XLA Modules:
  0.0 135.3 jit_solution(17756930626297761209)
XLA Ops:
  6.5 0.8 compare_and_fusion.1
  7.4 0.7 compare_select_fusion.3
  8.0 6.1 %gather_fusion = bf16[4,128,1024]{2,0,1:T(4,128)(2,1)} fusion(bf16[128,4,1024]{2,1,0:T(4,128)(2,1)} %param.6, s32[1024]{0:T(1024)S(1)} %pad_clamp_fusion.2), kind=kCustom, calls=%fused_computation | custom fusion | bytes 2097168 | tf_op jit(solution)/shard_map/jit(_take)/gather | solution.py:8
  14.1 1.7 %select_bitcast_fusion = bf16[128,4,1024]{2,1,0:T(4,128)(2,1)S(1)} fusion(bf16[4,128,1024]{2,0,1:T(4,128)(2,1)} %gather_fusion, pred[4]{0:T(512)(128)(4,1)S(1)} %compare_and_fusion.1), kind=kLoop, calls=%fused_computation.15 | loop fusion | flops 524288 | bytes 2097156 | tf_op jit(solution)/shard_map/jit(_take)/select_n | solution.py:8
  15.9 1.6 %fusion.16 = (bf16[128,1,1024]{2,1,0:T(2,128)(2,1)S(1)}, bf16[128,1,1024]{2,1,0:T(2,128)(2,1)S(1)}, bf16[128,1,1024]{2,1,0:T(2,128)(2,1)S(1)}, bf16[128,1,1024]{2,1,0:T(2,128)(2,1)S(1)}) fusion(bf16[128,4,1024]{2,1,0:T(4,128)(2,1)S(1)} %select_bitcast_fusion), kind=kLoop, calls=%fused_computation.34 | loop fusion | bytes 2097152 | tf_op jit(solution)/shard_map/split | solution.py:10
  17.4 0.2 copy_bitcast_fusion.2
  17.6 0.2 copy_bitcast_fusion
  17.8 0.1 pad_maximum_fusion
  17.9 0.0 copy-start.2
  17.9 32.0 %all_to_all.5 = bf16[4,128,1,1024]{3,1,2,0:T(8,128)(2,1)} all-to-all(bf16[4,128,1,1024]{3,1,2,0:T(8,128)(2,1)S(1)} %pad_maximum_fusion), channel_id=1, replica_groups=mesh['parts'=2,'blk'=4,'row'=2,'sub'=2] {'blk'}, dimensions={0} | all-to-all | bytes 2097152 | tf_op jit(solution)/shard_map/all_to_all | solution.py:10
  49.9 0.0 all-gather.3.cloned.1.call-update
  49.9 0.0 all-gather.5.cloned.1.call-start
  50.0 2.4 %scatter_custom_fusion = s32[512]{0:T(512)S(1)} fusion(s32[512]{0:T(512)S(1)} %compare_select_fusion.2, s32[512]{0:T(512)S(1)} %iota.3, s32[]{:T(128)} %constant.30.clone.1), kind=kCustom, calls=%fused_computation.31 | custom fusion | bytes 2052 | tf_op jit(solution)/shard_map/scatter | solution.py:21
  52.5 7.3 %all-gather.3.cloned.1.call-done = bf16[512,1,2048]{2,0,1:T(8,128)(2,1)} async-done(((bf16[512,1,1024]{2,0,1:T(8,128)(2,1)}), bf16[512,1,2048]{2,0,1:T(8,128)(2,1)}) %all-gather.3.cloned.1.call-update) | async-done | bytes 2097168 | tf_op jit(solution)/shard_map/all_gather | solution.py:16
  59.8 3.5 %fusion.8 = bf16[512,512]{1,0:T(8,128)(2,1)S(1)} fusion(bf16[1,512,2048]{2,1,0:T(8,128)(2,1)} %param.7, bf16[512,1,2048]{2,0,1:T(8,128)(2,1)} %all-gather.3.cloned.1.call-done), kind=kOutput, calls=%fused_computation.13 | convolution fusion | flops 1074003968 | bytes 4718592 | tf_op jit(solution)/shard_map/qsj,sij->qsi/dot_general | solution.py:14
  63.3 2.6 %gather_fusion.1 = bf16[512,512]{1,0:T(8,128)(2,1)} fusion(bf16[512,512]{1,0:T(8,128)(2,1)S(1)} %fusion.8, s32[1024]{0:T(1024)S(1)} %pad_clamp_fusion.1), kind=kCustom, calls=%fused_computation.1 | custom fusion | bytes 1050624 | tf_op jit(solution)/shard_map/jit(_take)/gather | solution.py:23
  65.9 2.0 %bitcast_select_fusion.2 = bf16[512,1,512]{2,0,1:T(8,128)(2,1)} fusion(bf16[512,512]{1,0:T(8,128)(2,1)} %gather_fusion.1, pred[512]{0:T(512)(128)(4,1)S(1)} %compare_and_fusion.2), kind=kLoop, calls=%fused_computation.16 | loop fusion | flops 262144 | bytes 1049088 | tf_op jit(solution)/shard_map/jit(_take)/select_n | solution.py:23
  67.9 0.0 all-gather.5.cloned.1.call-update
  67.9 0.0 reduce-scatter.2.cloned.1.call-start
  68.0 4.1 %gather_fusion.2 = bf16[640,2048]{1,0:T(8,128)(2,1)} fusion(bf16[640,2048]{1,0:T(8,128)(2,1)S(1)} %bitcast.36, s32[1024]{0:T(1024)S(1)} %pad_clamp_fusion), kind=kCustom, calls=%fused_computation.2 | custom fusion | bytes 5245440 | tf_op jit(solution)/shard_map/jit(_take)/gather | solution.py:24
  72.1 19.7 %all-gather.5.cloned.1.call-done = bf16[512,1,2048]{2,0,1:T(8,128)(2,1)} async-done(((bf16[512,1,512]{2,0,1:T(8,128)(2,1)}), bf16[512,1,2048]{2,0,1:T(8,128)(2,1)}) %all-gather.5.cloned.1.call-update) | async-done | bytes 2097168 | tf_op jit(solution)/shard_map/all_gather | solution.py:27
  91.8 5.4 %fusion = f32[512,640]{1,0:T(8,128)} fusion(bf16[640,2048]{1,0:T(8,128)(2,1)} %gather_fusion.2, pred[640]{0:T(1024)(128)(4,1)S(1)} %compare_and_fusion, bf16[512,1,2048]{2,0,1:T(8,128)(2,1)} %all-gather.5.cloned.1.call-done), kind=kOutput, calls=%fused_computation.4 | convolution fusion | flops 1343488000 | bytes 6029952 | tf_op jit(solution)/shard_map/qsk,rsk->qr/dot_general | solution.py:25
  97.2 0.0 reduce-scatter.2.cloned.1.call-update
  97.2 31.5 %reduce-scatter.2.cloned.1.call-done = f32[128,640]{1,0:T(8,128)} async-done(((f32[512,640]{1,0:T(8,128)}), f32[128,640]{1,0:T(8,128)}) %reduce-scatter.2.cloned.1.call-update) | async-done | bytes 327696 | tf_op jit(solution)/shard_map/reduce_scatter | solution.py:31
  (15 shorter events, 0.1 us)
Async XLA Ops:
  6.5 61.5 %copy-start = (bf16[640,1,2048]{2,0,1:T(8,128)(2,1)S(1)}, bf16[640,1,2048]{2,0,1:T(8,128)(2,1)}, u32[]{:S(2)}) copy-start(bf16[640,1,2048]{2,0,1:T(8,128)(2,1)} %param.8) | copy-start | bytes 7864324
  6.5 53.2 %all-gather.3.cloned.1.call-start = ((), (), s32[]{:S(2)}) async-start(), calls=%async_computation.2 | async-start | bytes 3145728 | tf_op jit(solution)/shard_map/all_gather | solution.py:16
  17.9 32.1 %copy-start.2 = (s32[512]{0:T(512)S(1)}, s32[512]{0:T(512)}, u32[]{:S(2)}) copy-start(s32[512]{0:T(512)} %param.9) | copy-start | bytes 6148
  49.9 41.9 %all-gather.5.cloned.1.call-start = ((), (), s32[]{:S(2)}) async-start(), calls=%async_computation.3 | async-start | bytes 2621440 | tf_op jit(solution)/shard_map/all_gather | solution.py:27
  63.3 4.7 %copy-start.1 = (s32[640]{0:T(1024)S(1)}, s32[640]{0:T(1024)}, u32[]{:S(2)}) copy-start(s32[640]{0:T(1024)} %param.11) | copy-start | bytes 7684
  67.9 60.8 %reduce-scatter.2.cloned.1.call-start = ((), (), s32[]{:S(2)}) async-start(), calls=%async_computation.4 | async-start | bytes 1638400 | tf_op jit(solution)/shard_map/reduce_scatter | solution.py:31
Sparse Core Ops, SparseCore 0:
  50.1 9.6 all-gather.2
  68.0 23.7 all-gather.4
  97.3 31.3 reduce-scatter.1
